TPU v7x, 32 devices: a whole 2x2x4 slice. The times are simulated.
32 devices in a mesh: tgt: 8 (over z, x), src: 4 (over y, core).
Axes of the slice: x: 2, y: 2, z: 4, core: 2. Of those that a mesh axis runs over, the one named last changes fastest.
Arguments:
- target_points: float32 [3, 8, 4096], P(None, None, 'src'), may hold values from 0 to 1
- source_points: float32 [3, 4096], P(None, 'tgt'), may hold values from 0 to 1
- charges: float32 [4096], P('tgt'), may hold values from 0.1 to 1
- sketch: bfloat16 [128, 4096], P(None, 'tgt'), may hold values from -0.09375 to 0.09375
- far_mask: int32 [8, 32], replicated, may hold values 0 or 1
Outputs:
- range_basis: bfloat16 [8, 4096, 128], P('tgt', 'src')
- far_factor: bfloat16 [8, 128, 4096], P('tgt', None, 'src')
All inputs are finite; a program needn't handle non-finite values.
Results may differ from a plain program's by a relative error of at most 0.02.
Values may be sent and summed in bfloat16 or wider, within the bound.
A program may use at most 128 MiB of HBM per device.

v0:
```python
import math

import jax
import jax.numpy as jnp
from jax import lax
from jax.sharding import PartitionSpec as P

SOFTENING = 0.0004
SHIFT_SCALE = 0.05


def kernel_tile(targets, sources, weight):
    delta_x = targets[0][:, None] - sources[0][None, :]
    delta_y = targets[1][:, None] - sources[1][None, :]
    delta_z = targets[2][:, None] - sources[2][None, :]
    distance2 = delta_x * delta_x + delta_y * delta_y + delta_z * delta_z + SOFTENING
    return (weight[None, :] / jnp.sqrt(distance2)).astype(jnp.bfloat16)


def sketch_product(kernel_block, columns):
    return lax.dot_general(
        kernel_block, columns, (((1,), (1,)), ((), ())), preferred_element_type=jnp.float32
    )


def lower_solve(lower_factor, right_side):
    return lax.linalg.triangular_solve(lower_factor, right_side, left_side=True, lower=True)


def body(target_points, source_points, charges, sketch, far_mask):
    tgt_count = lax.axis_size("tgt")
    src_count = lax.axis_size("src")
    tgt_index = lax.axis_index("tgt")
    block_rows = target_points.shape[1]
    rows_dev = target_points.shape[2]
    total_rows = rows_dev * src_count
    src_dev = source_points.shape[1]
    rank_width = sketch.shape[0]
    clusters = far_mask.shape[1]
    cluster_size = src_dev * tgt_count // clusters
    own_rows = block_rows // tgt_count
    own_targets = jnp.moveaxis(
        lax.dynamic_slice_in_dim(target_points, tgt_index * own_rows, own_rows, 1), 1, 0
    )
    own_mask = lax.dynamic_slice_in_dim(far_mask, tgt_index * own_rows, own_rows, 0)
    own_wide = jnp.repeat(own_mask, cluster_size, axis=1).astype(jnp.float32)
    packed = jnp.concatenate([source_points, charges[None, :]], axis=0)
    group_clusters = src_dev // cluster_size
    group_mask = lax.dynamic_slice_in_dim(far_mask, tgt_index * group_clusters, group_clusters, 1)
    weights = jnp.repeat(group_mask, cluster_size, axis=1).astype(jnp.float32) * charges[None, :]

    def per_row(row_inputs):
        targets, weight = row_inputs
        return sketch_product(kernel_tile(targets, source_points, weight), sketch)

    partial_value = lax.map(per_row, (jnp.moveaxis(target_points, 1, 0), weights))
    received = lax.all_to_all(
        partial_value.astype(jnp.bfloat16), "tgt", split_axis=0, concat_axis=0, tiled=True
    ).astype(partial_value.dtype)
    sketched = jnp.sum(received.reshape(tgt_count, own_rows, rows_dev, rank_width), axis=0)
    gram_local = jnp.einsum("bmr,bmq->brq", sketched, sketched, precision=lax.Precision.HIGHEST)
    gram_matrix = lax.psum(gram_local, "src")
    diag_shift = SHIFT_SCALE * jnp.trace(gram_matrix, axis1=1, axis2=2) / rank_width
    identity = jnp.eye(rank_width, dtype=jnp.float32)
    lower_factor = jnp.linalg.cholesky(gram_matrix + diag_shift[:, None, None] * identity)
    solved = jax.vmap(lower_solve)(lower_factor, jnp.swapaxes(sketched, 1, 2))
    range_basis = (math.sqrt(total_rows) * jnp.swapaxes(solved, 1, 2)).astype(jnp.bfloat16)
    inverse_rows = 1.0 / total_rows
    incoming = lax.all_gather(packed, "tgt", axis=1, tiled=True)
    shard_count = incoming.shape[1] // src_dev
    blocks = jnp.moveaxis(incoming.reshape(4, shard_count, src_dev), 1, 0)
    firsts = jnp.arange(shard_count, dtype=jnp.int32) * src_dev

    def per_block(block_inputs):
        points, block_first = block_inputs
        weights = lax.dynamic_slice_in_dim(own_wide, block_first, src_dev, 1) * points[3][None, :]

        def per_row(row_inputs):
            targets, weight, basis_rows = row_inputs
            kernel_block = kernel_tile(targets, points, weight)
            product = lax.dot_general(
                basis_rows,
                kernel_block,
                (((0,), (0,)), ((), ())),
                preferred_element_type=jnp.float32,
            )
            return product * inverse_rows

        return lax.map(per_row, (own_targets, weights, range_basis))

    projected = lax.map(per_block, (blocks, firsts))
    terms = jnp.moveaxis(projected, 0, 2).reshape(own_rows, rank_width, shard_count * src_dev)
    far_factor = lax.psum_scatter(
        terms.astype(jnp.bfloat16), "src", scatter_dimension=2, tiled=True
    )
    return (range_basis, far_factor)


def solution(mesh):
    placed = (P(None, None, "src"), P(None, "tgt"), P("tgt"), P(None, "tgt"), P())
    return jax.shard_map(
        body,
        mesh=mesh,
        in_specs=placed,
        out_specs=(P("tgt", "src", None), P("tgt", None, "src")),
        check_vma=False,
    )
```

profile of v0, /device:TPU:24, one launch (start us, length us, event | category | flops | bytes accessed | tf_op | source)
XLA Modules:
  0.0 217.6 jit_solution(4877415320611882699)
XLA Ops:
  8.0 1.0 copy.22
  9.8 29.1 %while.24 = (s32[]{:T(128)}, bf16[8,1024,128]{2,1,0:T(8,128)(2,1)}, f32[8,512]{1,0:T(8,128)S(1)}, f32[8,3,1024]{2,1,0:T(4,128)S(1)}, f32[3,512]{1,0:T(4,128)}, /...) while((s32[]{:T(128)}, bf16[8,1024,128]{2,1,0:T(8,128)(2,1)}, f32[8,512]{1,0:T(8,128)S(1)}, ...), condition=%wide.region_1.2_spmd, body=%wide.region_0.1_spmd.sunk | while | flops 139984896 | bytes 717453 | solution.py:56
  10.6 2.8 %fusion.43 = bf16[8,1024,128]{2,1,0:T(8,128)(2,1)} fusion(bf16[8,1024,128]{2,1,0:T(8,128)(2,1)} %get-tuple-element.265, s32[]{:T(128)} %get-tuple-element.264, bf16[128,512]{1,0:T(8,128)(2,1)} %get-tuple-element.279, f32[512]{0:T(512)S(1)} %bitcast.124, f32[1024]{0:T(1024)S(1)} %bitcast.119, f32[512]{0:T(512)S(1)} %bitcast.125, ...), kind=kOutput, calls=%fused_computation.2.clone.1 | convolution fusion | flops 139984896 | bytes 676352 | tf_op jit(solution)/shard_map/while/body/eval_jaxpr/dot_general | solution.py:21
  14.2 2.8 %fusion.43 = bf16[8,1024,128]{2,1,0:T(8,128)(2,1)} fusion(bf16[8,1024,128]{2,1,0:T(8,128)(2,1)} %get-tuple-element.265, s32[]{:T(128)} %get-tuple-element.264, bf16[128,512]{1,0:T(8,128)(2,1)} %get-tuple-element.279, f32[512]{0:T(512)S(1)} %bitcast.124, f32[1024]{0:T(1024)S(1)} %bitcast.119, f32[512]{0:T(512)S(1)} %bitcast.125, ...), kind=kOutput, calls=%fused_computation.2.clone.1 | convolution fusion | flops 139984896 | bytes 676352 | tf_op jit(solution)/shard_map/while/body/eval_jaxpr/dot_general | solution.py:21
  17.9 2.8 %fusion.43 = bf16[8,1024,128]{2,1,0:T(8,128)(2,1)} fusion(bf16[8,1024,128]{2,1,0:T(8,128)(2,1)} %get-tuple-element.265, s32[]{:T(128)} %get-tuple-element.264, bf16[128,512]{1,0:T(8,128)(2,1)} %get-tuple-element.279, f32[512]{0:T(512)S(1)} %bitcast.124, f32[1024]{0:T(1024)S(1)} %bitcast.119, f32[512]{0:T(512)S(1)} %bitcast.125, ...), kind=kOutput, calls=%fused_computation.2.clone.1 | convolution fusion | flops 139984896 | bytes 676352 | tf_op jit(solution)/shard_map/while/body/eval_jaxpr/dot_general | solution.py:21
  21.5 2.8 %fusion.43 = bf16[8,1024,128]{2,1,0:T(8,128)(2,1)} fusion(bf16[8,1024,128]{2,1,0:T(8,128)(2,1)} %get-tuple-element.265, s32[]{:T(128)} %get-tuple-element.264, bf16[128,512]{1,0:T(8,128)(2,1)} %get-tuple-element.279, f32[512]{0:T(512)S(1)} %bitcast.124, f32[1024]{0:T(1024)S(1)} %bitcast.119, f32[512]{0:T(512)S(1)} %bitcast.125, ...), kind=kOutput, calls=%fused_computation.2.clone.1 | convolution fusion | flops 139984896 | bytes 676352 | tf_op jit(solution)/shard_map/while/body/eval_jaxpr/dot_general | solution.py:21
  25.1 2.8 %fusion.43 = bf16[8,1024,128]{2,1,0:T(8,128)(2,1)} fusion(bf16[8,1024,128]{2,1,0:T(8,128)(2,1)} %get-tuple-element.265, s32[]{:T(128)} %get-tuple-element.264, bf16[128,512]{1,0:T(8,128)(2,1)} %get-tuple-element.279, f32[512]{0:T(512)S(1)} %bitcast.124, f32[1024]{0:T(1024)S(1)} %bitcast.119, f32[512]{0:T(512)S(1)} %bitcast.125, ...), kind=kOutput, calls=%fused_computation.2.clone.1 | convolution fusion | flops 139984896 | bytes 676352 | tf_op jit(solution)/shard_map/while/body/eval_jaxpr/dot_general | solution.py:21
  28.8 2.8 %fusion.43 = bf16[8,1024,128]{2,1,0:T(8,128)(2,1)} fusion(bf16[8,1024,128]{2,1,0:T(8,128)(2,1)} %get-tuple-element.265, s32[]{:T(128)} %get-tuple-element.264, bf16[128,512]{1,0:T(8,128)(2,1)} %get-tuple-element.279, f32[512]{0:T(512)S(1)} %bitcast.124, f32[1024]{0:T(1024)S(1)} %bitcast.119, f32[512]{0:T(512)S(1)} %bitcast.125, ...), kind=kOutput, calls=%fused_computation.2.clone.1 | convolution fusion | flops 139984896 | bytes 676352 | tf_op jit(solution)/shard_map/while/body/eval_jaxpr/dot_general | solution.py:21
  32.4 2.8 %fusion.43 = bf16[8,1024,128]{2,1,0:T(8,128)(2,1)} fusion(bf16[8,1024,128]{2,1,0:T(8,128)(2,1)} %get-tuple-element.265, s32[]{:T(128)} %get-tuple-element.264, bf16[128,512]{1,0:T(8,128)(2,1)} %get-tuple-element.279, f32[512]{0:T(512)S(1)} %bitcast.124, f32[1024]{0:T(1024)S(1)} %bitcast.119, f32[512]{0:T(512)S(1)} %bitcast.125, ...), kind=kOutput, calls=%fused_computation.2.clone.1 | convolution fusion | flops 139984896 | bytes 676352 | tf_op jit(solution)/shard_map/while/body/eval_jaxpr/dot_general | solution.py:21
  36.0 2.8 %fusion.43 = bf16[8,1024,128]{2,1,0:T(8,128)(2,1)} fusion(bf16[8,1024,128]{2,1,0:T(8,128)(2,1)} %get-tuple-element.265, s32[]{:T(128)} %get-tuple-element.264, bf16[128,512]{1,0:T(8,128)(2,1)} %get-tuple-element.279, f32[512]{0:T(512)S(1)} %bitcast.124, f32[1024]{0:T(1024)S(1)} %bitcast.119, f32[512]{0:T(512)S(1)} %bitcast.125, ...), kind=kOutput, calls=%fused_computation.2.clone.1 | convolution fusion | flops 139984896 | bytes 676352 | tf_op jit(solution)/shard_map/while/body/eval_jaxpr/dot_general | solution.py:21
  38.8 6.2 %all-to-all-start = ((bf16[8,1024,128]{2,1,0:T(8,128)(2,1)}), bf16[8,1024,128]{2,1,0:T(8,128)(2,1)S(1)}, u32[]{:S(2)}, u32[]{:S(2)}) async-start(bf16[8,1024,128]{2,1,0:T(8,128)(2,1)} %get-tuple-element.89), calls=%async_computation | async-start | bytes 4194304 | tf_op jit(solution)/shard_map/all_to_all | solution.py:57
  45.7 0.9 dynamic-slice_bitcast_fusion.1
  46.6 45.1 %all-to-all-done = bf16[8,1024,128]{2,1,0:T(8,128)(2,1)S(1)} async-done(((bf16[8,1024,128]{2,1,0:T(8,128)(2,1)}), bf16[8,1024,128]{2,1,0:T(8,128)(2,1)S(1)}, u32[]{:S(2)}, u32[]{:S(2)}) %all-to-all-start) | async-done | bytes 2097184 | tf_op jit(solution)/shard_map/all_to_all | solution.py:57
  92.0 1.6 convolution_bitcast_fusion.1
  93.7 28.8 %all_gather.3 = f32[4,4096]{1,0:T(4,128)S(1)} all-gather(f32[4,512]{1,0:T(4,128)S(1)} %pad_maximum_fusion), channel_id=1, replica_groups=mesh['tgt'=8,'src'=4] {'tgt'}, dimensions={1}, use_global_device_ids=true | all-gather | bytes 73728 | tf_op jit(solution)/shard_map/all_gather | solution.py:69
  122.6 2.4 %all-reduce.2.cloned.1.call-done = f32[1,128,128]{2,1,0:T(8,128)} async-done(((f32[1,128,128]{2,1,0:T(8,128)}), f32[1,128,128]{2,1,0:T(8,128)}) %all-reduce.2.cloned.1.call-update) | async-done | bytes 65552 | tf_op jit(solution)/shard_map/psum | solution.py:62
  125.0 1.5 select_reduce_fusion.1
  127.1 0.9 select_add_fusion
  128.1 0.9 fusion.26
  128.9 11.7 %custom-call.7 = f32[1,128,128]{2,1,0:T(8,128)S(1)} custom-call(f32[1,128,128]{2,1,0:T(8,128)S(1)} %fusion.26), custom_call_target="Cholesky" | custom-call | tf_op jit(solution)/shard_map/jit(cholesky)/cholesky | solution.py:65
  142.0 9.8 %custom-call.8 = f32[1,1,128,128]{2,3,1,0:T(8,128)S(1)} custom-call(f32[1,1,128,128]{3,2,1,0:T(8,128)S(1)} %fusion.24), custom_call_target="InvertDiagBlocksLowerTriangular" | custom-call | tf_op jit(solution)/shard_map/vmap()/triangular_solve | solution.py:27
  152.7 31.6 %while.25 = (s32[]{:T(128)}, bf16[8,1,128,512]{2,3,1,0:T(8,128)(2,1)S(1)}, s32[8]{0:T(128)S(1)}, f32[1,4096]{1,0:T(1,128)S(1)}, f32[8,4,512]{2,1,0:T(4,128)S(1)}...) while((s32[]{:T(128)}, ...), condition=%wide.region_8.9_spmd, body=%wide.region_7.8_spmd.sunk | while | flops 140050944 | bytes 588011 | solution.py:91
  155.3 1.3 fusion.47
  159.3 1.3 fusion.47
  163.2 1.3 fusion.47
  167.2 1.3 fusion.47
  171.2 1.3 fusion.47
  175.1 1.3 fusion.47
  179.1 1.3 fusion.47
  183.0 1.3 fusion.47
  184.3 1.3 copy.20
  185.7 25.1 %reduce-scatter.2.cloned.1.call-done = bf16[1,128,1024]{2,1,0:T(8,128)(2,1)} async-done(((bf16[1,128,4096]{2,1,0:T(8,128)(2,1)}), bf16[1,128,1024]{2,1,0:T(8,128)(2,1)}) %reduce-scatter.2.cloned.1.call-update) | async-done | bytes 262160 | tf_op jit(solution)/shard_map/reduce_scatter | solution.py:93
  (75 shorter events, 17.2 us)
Async XLA Ops:
  38.8 6.9 %copy-start.1 = (f32[3,512]{1,0:T(4,128)S(1)}, f32[3,512]{1,0:T(4,128)}, u32[]{:S(2)}) copy-start(f32[3,512]{1,0:T(4,128)} %get-tuple-element.334) | copy-start | bytes 18436
  38.8 6.9 %copy-start.2 = (f32[512]{0:T(512)S(1)}, f32[512]{0:T(512)}, u32[]{:S(2)}) copy-start(f32[512]{0:T(512)} %param.11) | copy-start | bytes 6148
  38.8 52.8 %all-to-all-start = ((bf16[8,1024,128]{2,1,0:T(8,128)(2,1)}), bf16[8,1024,128]{2,1,0:T(8,128)(2,1)S(1)}, u32[]{:S(2)}, u32[]{:S(2)}) async-start(bf16[8,1024,128]{2,1,0:T(8,128)(2,1)} %get-tuple-element.89), calls=%async_computation | async-start | bytes 4194304 | tf_op jit(solution)/shard_map/all_to_all | solution.py:57
  45.0 80.0 %all-reduce.2.cloned.1.call-start = ((), (), s32[]{:S(2)}) async-start(), calls=%async_computation.2 | async-start | bytes 131072 | tf_op jit(solution)/shard_map/psum | solution.py:62
  93.7 117.1 %reduce-scatter.2.cloned.1.call-start = ((), (), s32[]{:S(2)}) async-start(), calls=%async_computation.3 | async-start | bytes 1310720 | tf_op jit(solution)/shard_map/reduce_scatter | solution.py:93
  184.3 26.4 %copy-start = (bf16[1,1024,128]{2,1,0:T(8,128)(2,1)}, bf16[1,1024,128]{2,1,0:T(8,128)(2,1)S(1)}, u32[]{:S(2)}) copy-start(bf16[1,1024,128]{2,1,0:T(8,128)(2,1)S(1)} %get-tuple-element.333) | copy-start | bytes 786436
Sparse Core Ops, SparseCore 0:
  93.8 31.1 all-reduce.1
  185.8 24.8 reduce-scatter.1
where the time goes:
time: 221 us; the launch traced here: 218 us
  waiting for transfers between devices  72.6 us (33%)
  matrix products  35 us (16%)
  other arithmetic  29.2 us (13%)
  blocking collectives  28.8 us (13%)
  loops' own time  15.8 us (7%)
  local copies, waits for them, and re-layouts  15.1 us (7%)
  between operations  14.8 us (7%)
  starting transfers between devices  6.2 us (3%)
    all_to_all x1, waiting for transfers between devices, body(): lax.all_to_all(partial_value.astype(jnp.bfloat16), 'tgt', split_axis=0, c...  45.1 us
    all_gather x1, blocking collectives, body(): incoming = lax.all_gather(packed, 'tgt', axis=1, tiled=True)  28.8 us
    reduce_scatter x1, waiting for transfers between devices, body(): lax.psum_scatter(terms.astype(jnp.bfloat16), 'src', scatter_dimension=2,...  25.1 us
    dot_general x8, matrix products, sketch_product(): lax.dot_general(kernel_block, columns, (((1,), (1,)), ((), ())), preferre...  22.4 us
    another operation x1, loops' own time, body(): projected = lax.map(per_block, (blocks, firsts))  15.8 us
    another operation x3, other arithmetic, body(): jnp.linalg.cholesky(gram_matrix + diag_shift[:, None, None] * identity)  12.4 us
    another operation x2, other arithmetic, lower_solve(): lax.linalg.triangular_solve(lower_factor, right_side, left_side=True, low...  10.5 us
    dot_general x8, matrix products, per_row(): lax.dot_general(basis_rows, kernel_block, (((0,), (0,)), ((), ())), prefe...  10.3 us
  transfers between devices with their start and end apart: 3, of which 3 were waited for; matrix products, arithmetic and copies ran while one was open for 1% of the time, Pallas kernels for 0%

commit v1 on v0

v1 whole, which is shorter than its diff:
```python
import functools
import math

import jax
import jax.numpy as jnp
from jax import lax
from jax.experimental import pallas as pl
from jax.experimental.pallas import tpu as pltpu
from jax.sharding import PartitionSpec as P

SOFTENING = 0.0004
SHIFT_SCALE = 0.05
MESH = pl.DeviceIdType.MESH
HIGHEST = lax.Precision.HIGHEST
F32 = jnp.float32
BF16 = jnp.bfloat16
VMEM_LIMIT = 56 << 20


def remote(src, dst, send_sem, recv_sem, device):
    return pltpu.make_async_remote_copy(
        src_ref=src, dst_ref=dst, send_sem=send_sem, recv_sem=recv_sem,
        device_id=device, device_id_type=MESH,
    )


def sketch_kernel(
    n_t, n_s, cluster, targets_ref, points_ref, charges_ref, sketch_ref, mask_ref,
    kernel_out, sketched_ref, gram_ref,
    packed, columns, kernel_all, target_cols, grams,
    pk_send, pk_recv, sk_send, sk_recv, mate_send, mate_recv, g_send, g_recv, out_sem,
):
    t = lax.axis_index("tgt")
    s = lax.axis_index("src")
    core = s % 2
    mate = s + 1 - 2 * core
    rank, width = sketch_ref.shape
    rows = targets_ref.shape[2]
    half = rank // 2

    barrier = pltpu.get_barrier_semaphore()
    for d in range(1, n_t):
        pl.semaphore_signal(barrier, inc=1, device_id=((t + d) % n_t, s), device_id_type=MESH)
    for d in range(1, n_s):
        pl.semaphore_signal(barrier, inc=1, device_id=(t, (s + d) % n_s), device_id_type=MESH)

    packed[t, 0:3, :] = points_ref[...]
    packed[t, 3:4, :] = charges_ref[...]
    columns[t] = sketch_ref[...]
    pl.semaphore_wait(barrier, n_t + n_s - 2)

    def halves(owner, which):
        return columns.at[owner, pl.ds(pl.multiple_of(which * half, half), half)]

    def packed_copy(d):
        return remote(packed.at[t], packed.at[t], pk_send.at[d], pk_recv.at[t], ((t + d) % n_t, s))

    def half_copy(d):
        return remote(halves(t, core), halves(t, core), sk_send.at[d], sk_recv.at[t], ((t + d) % n_t, s))

    def mate_copy(owner):
        return remote(halves(owner, core), halves(owner, core), mate_send.at[owner], mate_recv.at[owner], (t, mate))

    def out_copy(owner):
        return pltpu.make_async_copy(kernel_all.at[owner], kernel_out.at[owner], out_sem.at[owner])

    for d in range(1, n_t):
        packed_copy(d).start()
    for d in range(1, n_t):
        half_copy(d).start()

    lanes = 128
    stacked = jnp.concatenate(
        [targets_ref[0, pl.ds(t, 1), :], targets_ref[1, pl.ds(t, 1), :], targets_ref[2, pl.ds(t, 1), :],
         jnp.zeros((5, rows), F32)], axis=0)
    for first in range(0, rows, 128):
        block = jnp.concatenate([stacked[:, first:first + 128], jnp.zeros((120, 128), F32)], axis=0).T
        for axis in range(3):
            target_cols[axis, first:first + 128, :] = jnp.broadcast_to(block[:, axis:axis + 1], (128, lanes))
    sketched_ref[...] = jnp.zeros_like(sketched_ref)

    chunk = 256
    sub = 64

    def sweep(owner, previous):
        sx, sy, sz = packed[owner, 0:1, :], packed[owner, 1:2, :], packed[owner, 2:3, :]
        charge = packed[owner, 3:4, :]
        weights = []
        for piece in range(width // lanes):
            near = mask_ref[t, owner * (width // cluster) + piece * lanes // cluster]
            weights.append(charge[:, piece * lanes:(piece + 1) * lanes] * near.astype(F32))

        def step(index, carry):
            base = pl.multiple_of(index * chunk, chunk)
            for inner in range(chunk // sub):
                at = pl.ds(base + inner * sub, sub)
                tx, ty, tz = target_cols[0, at, :], target_cols[1, at, :], target_cols[2, at, :]
                for piece in range(width // lanes):
                    cut = slice(piece * lanes, (piece + 1) * lanes)
                    dx = tx - sx[:, cut]
                    dy = ty - sy[:, cut]
                    dz = tz - sz[:, cut]
                    distance2 = dx * dx + dy * dy + dz * dz + SOFTENING
                    kernel_all[owner, at, cut] = (weights[piece] * lax.rsqrt(distance2)).astype(BF16)
            if previous is not None:
                at = pl.ds(base, chunk)
                sketched_ref[at, :] += lax.dot_general(
                    kernel_all[previous, at, :], columns[previous], (((1,), (1,)), ((), ())),
                    preferred_element_type=F32)
            return carry

        lax.fori_loop(0, rows // chunk, step, 0)

    sweep(t, None)
    out_copy(t).start()

    def visit(d, carry):
        owner = (t + n_t - d) % n_t
        previous = (t + n_t - d + 1) % n_t
        pltpu.make_async_copy(packed.at[owner], packed.at[owner], pk_recv.at[owner]).wait()

        @pl.when(d >= 2)
        def _():
            pltpu.make_async_copy(halves(previous, 1 - core), halves(previous, 1 - core), mate_recv.at[previous]).wait()

        sweep(owner, previous)
        out_copy(owner).start()
        pltpu.make_async_copy(halves(owner, core), halves(owner, core), sk_recv.at[owner]).wait()
        mate_copy(owner).start()
        return carry

    lax.fori_loop(1, n_t, visit, 0)
    last = (t + 1) % n_t
    pltpu.make_async_copy(halves(last, 1 - core), halves(last, 1 - core), mate_recv.at[last]).wait()

    def finish(index, carry):
        at = pl.ds(pl.multiple_of(index * chunk, chunk), chunk)
        sketched_ref[at, :] += lax.dot_general(
            kernel_all[last, at, :], columns[last], (((1,), (1,)), ((), ())), preferred_element_type=F32)
        return carry

    lax.fori_loop(0, rows // chunk, finish, 0)
    sketched = sketched_ref[...]
    grams[s] = jnp.dot(sketched.T, sketched, precision=HIGHEST, preferred_element_type=F32)

    def gram_copy(d):
        return remote(grams.at[s], grams.at[s], g_send.at[d], g_recv.at[s], (t, (s + d) % n_s))

    for d in range(1, n_s):
        gram_copy(d).start()
    for d in range(1, n_s):
        owner = (s + d) % n_s
        pltpu.make_async_copy(grams.at[owner], grams.at[owner], g_recv.at[owner]).wait()
    total = grams[0]
    for d in range(1, n_s):
        total = total + grams[d]
    gram_ref[...] = total

    for d in range(1, n_s):
        gram_copy(d).wait_send()
    for d in range(1, n_t):
        packed_copy(d).wait_send()
        half_copy(d).wait_send()
        mate_copy((t + d) % n_t).wait_send()
    for d in range(n_t):
        out_copy((t + d) % n_t).wait()


def basis_kernel(total_rows, gram_ref, sketched_ref, basis_ref, flipped_ref, work, inverse):
    rank = gram_ref.shape[0]
    gram = gram_ref[...]
    row = lax.broadcasted_iota(jnp.int32, (rank, rank), 0)
    col = lax.broadcasted_iota(jnp.int32, (rank, rank), 1)
    eye = row == col
    trace = jnp.sum(jnp.where(eye, gram, 0.0))
    work[...] = gram + jnp.where(eye, SHIFT_SCALE * trace / rank, 0.0)
    inverse[...] = jnp.where(eye, 1.0, 0.0)
    size = 16
    local = lax.broadcasted_iota(jnp.int32, (size, rank), 0)
    for first in range(0, rank, size):
        panel = work[first:first + size, :]
        inv_panel = inverse[first:first + size, :]
        cols = [jnp.broadcast_to(panel[:, first + i:first + i + 1], (size, rank)) for i in range(size)]
        for i in range(size):
            pivot = jnp.broadcast_to(cols[i][i:i + 1, :], (size, rank))
            scale = lax.rsqrt(pivot)
            scale = scale * (1.5 - 0.5 * pivot * scale * scale)
            factor = jnp.where(local > i, cols[i] * scale, 0.0)
            panel_row = panel[i:i + 1, :] * scale
            inv_row = inv_panel[i:i + 1, :] * scale
            panel = jnp.where(local == i, panel_row, panel - factor * panel_row)
            inv_panel = jnp.where(local == i, inv_row, inv_panel - factor * inv_row)
            for j in range(i + 1, size):
                cols[j] = cols[j] - factor * (cols[j][i:i + 1, :] * scale)
        inverse[first:first + size, :] = inv_panel
        rest = first + size
        if rest < rank:
            both = jnp.concatenate([panel, inv_panel], axis=1)
            update = lax.dot_general(
                panel, both, (((0,), (0,)), ((), ())), precision=HIGHEST, preferred_element_type=F32)
            work[rest:, :] -= update[rest:, :rank]
            inverse[rest:, :] -= update[rest:, rank:]
    basis = math.sqrt(total_rows) * lax.dot_general(
        sketched_ref[...], inverse[...], (((1,), (1,)), ((), ())),
        precision=HIGHEST, preferred_element_type=F32)
    basis_ref[...] = basis.astype(BF16)
    flipped_ref[...] = basis.T.astype(BF16)


def project_kernel(
    n_t, n_s, scale, flipped_ref, kernel_in, out_ref,
    kernel_all, partial, to_mate, from_mate, to_far, from_far,
    in_sem, mate_send, mate_recv, far_send, far_recv,
):
    t = lax.axis_index("tgt")
    s = lax.axis_index("src")
    core = s % 2
    y = s // 2
    n_y = n_s // 2
    mate = s + 1 - 2 * core
    per = n_t // n_s
    width = kernel_all.shape[2]

    barrier = pltpu.get_barrier_semaphore()
    pl.semaphore_signal(barrier, inc=1, device_id=(t, mate), device_id_type=MESH)
    for d in range(1, n_y):
        pl.semaphore_signal(barrier, inc=1, device_id=(t, ((y + d) % n_y) * 2 + core), device_id_type=MESH)

    def in_copy(block):
        return pltpu.make_async_copy(kernel_in.at[block], kernel_all.at[block], in_sem.at[block])

    order = [((y + d) % n_y) * 2 + 1 - core for d in range(1, n_y)]
    order += [((y + d) % n_y) * 2 + core for d in range(1, n_y)]
    order += [mate, s]
    for dest in order:
        for piece in range(per):
            in_copy(dest * per + piece).start()
    pl.semaphore_wait(barrier, n_y)

    def product(dest, piece):
        block = dest * per + piece
        in_copy(block).wait()
        return scale * jnp.dot(flipped_ref[...], kernel_all[block], preferred_element_type=F32)

    def mate_copy(d):
        return remote(to_mate.at[d], from_mate.at[d], mate_send.at[d], mate_recv.at[d], (t, mate))

    def far_copy(d):
        return remote(to_far.at[d], from_far.at[d], far_send.at[d], far_recv.at[d],
                      (t, ((y + d) % n_y) * 2 + core))

    def cut(piece):
        return slice(piece * width, (piece + 1) * width)

    for d in range(1, n_y):
        for piece in range(per):
            to_mate[d, :, cut(piece)] = product(order[d - 1], piece).astype(BF16)
        mate_copy(d).start()
    for d in range(1, n_y):
        for piece in range(per):
            partial[d, :, cut(piece)] = product(order[n_y - 2 + d], piece)
    for d in range(1, n_y):
        mate_copy(d).wait_recv()
        to_far[d] = (partial[d] + from_mate[d].astype(F32)).astype(BF16)
        far_copy(d).start()
    for piece in range(per):
        to_mate[0, :, cut(piece)] = product(mate, piece).astype(BF16)
    mate_copy(0).start()
    for piece in range(per):
        partial[0, :, cut(piece)] = product(s, piece)
    mate_copy(0).wait_recv()
    total = partial[0] + from_mate[0].astype(F32)
    for d in range(1, n_y):
        far_copy(d).wait_recv()
        total = total + from_far[d].astype(F32)
    out_ref[...] = total.astype(BF16)
    for d in range(n_y):
        mate_copy(d).wait_send()
    for d in range(1, n_y):
        far_copy(d).wait_send()


def body(target_points, source_points, charges, sketch, far_mask):
    n_t = lax.axis_size("tgt")
    n_s = lax.axis_size("src")
    rows = target_points.shape[2]
    total_rows = rows * n_s
    width = source_points.shape[1]
    rank = sketch.shape[0]
    cluster = width * n_t // far_mask.shape[1]
    vmem = pl.BlockSpec(memory_space=pltpu.VMEM)
    smem = pl.BlockSpec(memory_space=pltpu.SMEM)
    hbm = pl.BlockSpec(memory_space=pl.ANY)
    dma = pltpu.SemaphoreType.DMA
    kernel_all, sketched, gram = pl.pallas_call(
        functools.partial(sketch_kernel, n_t, n_s, cluster),
        out_shape=(
            jax.ShapeDtypeStruct((n_t, rows, width), BF16),
            jax.ShapeDtypeStruct((rows, rank), F32),
            jax.ShapeDtypeStruct((rank, rank), F32),
        ),
        in_specs=[vmem, vmem, vmem, vmem, smem],
        out_specs=(hbm, vmem, vmem),
        scratch_shapes=[
            pltpu.VMEM((n_t, 4, width), F32),
            pltpu.VMEM((n_t, rank, width), BF16),
            pltpu.VMEM((n_t, rows, width), BF16),
            pltpu.VMEM((3, rows, 128), F32),
            pltpu.VMEM((n_s, rank, rank), F32),
            dma((n_t,)), dma((n_t,)), dma((n_t,)), dma((n_t,)), dma((n_t,)), dma((n_t,)),
            dma((n_s,)), dma((n_s,)), dma((n_t,)),
        ],
        compiler_params=pltpu.CompilerParams(
            collective_id=0, has_side_effects=True, vmem_limit_bytes=VMEM_LIMIT),
        name="sketch",
    )(target_points, source_points, charges[None, :], sketch, far_mask)
    basis, flipped = pl.pallas_call(
        functools.partial(basis_kernel, total_rows),
        out_shape=(
            jax.ShapeDtypeStruct((rows, rank), BF16),
            jax.ShapeDtypeStruct((rank, rows), BF16),
        ),
        in_specs=[vmem, vmem],
        out_specs=(vmem, vmem),
        scratch_shapes=[pltpu.VMEM((rank, rank), F32), pltpu.VMEM((rank, rank), F32)],
        name="basis",
    )(gram, sketched)
    n_y = n_s // 2
    span = width * n_t // n_s
    factor = pl.pallas_call(
        functools.partial(project_kernel, n_t, n_s, 1.0 / total_rows),
        out_shape=jax.ShapeDtypeStruct((rank, span), BF16),
        in_specs=[vmem, hbm],
        out_specs=vmem,
        scratch_shapes=[
            pltpu.VMEM((n_t, rows, width), BF16),
            pltpu.VMEM((n_y, rank, span), F32),
            pltpu.VMEM((n_y, rank, span), BF16),
            pltpu.VMEM((n_y, rank, span), BF16),
            pltpu.VMEM((n_y, rank, span), BF16),
            pltpu.VMEM((n_y, rank, span), BF16),
            dma((n_t,)), dma((n_y,)), dma((n_y,)), dma((n_y,)), dma((n_y,)),
        ],
        compiler_params=pltpu.CompilerParams(
            collective_id=1, has_side_effects=True, vmem_limit_bytes=VMEM_LIMIT),
        name="project",
    )(flipped, kernel_all)
    return basis[None], factor[None]


def solution(mesh):
    placed = (P(None, None, "src"), P(None, "tgt"), P("tgt"), P(None, "tgt"), P())
    return jax.shard_map(
        body,
        mesh=mesh,
        in_specs=placed,
        out_specs=(P("tgt", "src", None), P("tgt", None, "src")),
        check_vma=False,
    )
```

time: 221 us -> 60.1 us (0.27); the launches traced: 218 us -> 59.1 us
  waiting for transfers between devices: 72.6 us -> 0 us
  Pallas kernels: 0 us -> 56.8 us
  matrix products: 35 us -> 0 us
  other arithmetic: 29.2 us -> 0 us
  blocking collectives: 28.8 us -> 0 us
  loops' own time: 15.8 us -> 0 us
  between operations: 14.8 us -> 0.65 us
  local copies, waits for them, and re-layouts: 15.1 us -> 1.67 us
  starting transfers between devices: 6.2 us -> 0 us
    pallas_call x0 -> x3, Pallas kernels: none -> 56.8 us  [the longest x1 36.1 us: body(): pl.pallas_call(functools.partial(sketch_kernel, n_t, n_s, cluster), out_s...]
    all_to_all x1 -> x0, waiting for transfers between devices: 45.1 us -> none  [body(): lax.all_to_all(partial_value.astype(jnp.bfloat16), 'tgt', split_axis=0, c...]
    dot_general x17 -> x0, matrix products: 34.3 us -> none  [the longest x8 22.4 us: sketch_product(): lax.dot_general(kernel_block, columns, (((1,), (1,)), ((), ())), preferre...]
    all_gather x1 -> x0, blocking collectives: 28.8 us -> none  [body(): incoming = lax.all_gather(packed, 'tgt', axis=1, tiled=True)]
    reduce_scatter x1 -> x0, waiting for transfers between devices: 25.1 us -> none  [body(): lax.psum_scatter(terms.astype(jnp.bfloat16), 'src', scatter_dimension=2,...]
    another operation x5 -> x0, other arithmetic: 22.9 us -> none  [the longest x3 12.4 us: body(): jnp.linalg.cholesky(gram_matrix + diag_shift[:, None, None] * identity)]
    another operation x2 -> x0, loops' own time: 15.8 us -> none  [the longest x1 15.8 us: body(): projected = lax.map(per_block, (blocks, firsts))]
    slice x32 -> x0, local copies, waits for them, and re-layouts: 6.82 us -> none  [kernel_tile(): delta_x = targets[0][:, None] - sources[0][None, :]]
  transfers between devices with their start and end apart: 3 -> 0, of which waited for: 3 -> 0; matrix products, arithmetic and copies ran while one was open for 1% -> 0% of each run, Pallas kernels for 0% -> 0%
where the time goes in v1:
time: 60.1 us; the launch traced here: 59.1 us
  Pallas kernels  56.8 us (95%)
  local copies, waits for them, and re-layouts  1.67 us (3%)
  between operations  0.65 us (1%)
    pallas_call x1, Pallas kernels, body(): pl.pallas_call(functools.partial(sketch_kernel, n_t, n_s, cluster), out_s...  36.1 us
    pallas_call x1, Pallas kernels, body(): pl.pallas_call(functools.partial(project_kernel, n_t, n_s, 1.0 / total_ro...  12.6 us
    pallas_call x1, Pallas kernels, body(): pl.pallas_call(functools.partial(basis_kernel, total_rows), out_shape=(ja...  8.14 us
    unnamed x1, local copies, waits for them, and re-layouts  1.67 us

profile of v1, /device:TPU:24, one launch (start us, length us, event | category | flops | bytes accessed | tf_op | source)
XLA Modules:
  0.0 59.1 jit_solution(1949011443844810882)
XLA Ops:
  0.6 36.1 %sketch.1 = (bf16[8,1024,512]{2,1,0:T(8,128)(2,1)}, f32[1024,128]{1,0:T(8,128)}, f32[128,128]{1,0:T(8,128)}) custom-call(f32[3,8,1024]{2,1,0:T(8,128)} %targets_ref.1, f32[3,512]{1,0:T(4,128)} %points_ref.1, f32[1,512]{1,0:T(1,128)} %bitcast.4, bf16[128,512]{1,0:T(8,128)(2,1)} %sketch_ref.1, s32[8,32]{1,0:T(8,128)} %mask_ref.1), custom_call_target="tpu_custom_call" | custom-call | tf_op jit(solution)/shard_map/sketch/pallas_call | solution.py:295
  36.7 8.1 %basis.1 = (bf16[1024,128]{1,0:T(8,128)(2,1)}, bf16[128,1024]{1,0:T(8,128)(2,1)}) custom-call(f32[128,128]{1,0:T(8,128)} %get-tuple-element.7.gram_ref, f32[1024,128]{1,0:T(8,128)} %get-tuple-element.8.sketched_ref), custom_call_target="tpu_custom_call" | custom-call | tf_op jit(solution)/shard_map/basis/pallas_call | solution.py:317
  44.8 12.6 %project.1 = bf16[128,1024]{1,0:T(8,128)(2,1)} custom-call(bf16[128,1024]{1,0:T(8,128)(2,1)} %get-tuple-element.10.flipped_ref, bf16[8,1024,512]{2,1,0:T(8,128)(2,1)} %get-tuple-element.11.kernel_in), custom_call_target="tpu_custom_call" | custom-call | tf_op jit(solution)/shard_map/project/pallas_call | solution.py:330
  57.4 1.7 %copy.8 = bf16[1,128,1024]{2,1,0:T(8,128)(2,1)} copy(bf16[1,128,1024]{2,1,0:T(8,128)(2,1)} %bitcast.3) | data formatting | bytes 524288

commit v2 on v1

--- a/solution.py
+++ b/solution.py
@@ -79,7 +79,7 @@
             target_cols[axis, first:first + 128, :] = jnp.broadcast_to(block[:, axis:axis + 1], (128, lanes))
     sketched_ref[...] = jnp.zeros_like(sketched_ref)
 
-    chunk = 256
+    chunk = rows
     sub = 64
 
     def sweep(owner, previous):
@@ -111,35 +111,68 @@
 
         lax.fori_loop(0, rows // chunk, step, 0)
 
+    lag = 2
+    ahead = 2
+
+    def at_distance(d):
+        return (t + n_t - d) % n_t
+
+    def forward(d):
+        owner = at_distance(d)
+        pltpu.make_async_copy(halves(owner, core), halves(owner, core), sk_recv.at[owner]).wait()
+        mate_copy(owner).start()
+
+    def complete(d):
+        owner = at_distance(d)
+        pltpu.make_async_copy(halves(owner, 1 - core), halves(owner, 1 - core), mate_recv.at[owner]).wait()
+
     sweep(t, None)
     out_copy(t).start()
 
     def visit(d, carry):
-        owner = (t + n_t - d) % n_t
-        previous = (t + n_t - d + 1) % n_t
+        owner = at_distance(d)
         pltpu.make_async_copy(packed.at[owner], packed.at[owner], pk_recv.at[owner]).wait()
 
-        @pl.when(d >= 2)
+        @pl.when(d > lag)
         def _():
-            pltpu.make_async_copy(halves(previous, 1 - core), halves(previous, 1 - core), mate_recv.at[previous]).wait()
-
-        sweep(owner, previous)
+            complete(d - lag)
+
+        @pl.when(d >= lag)
+        def _():
+            sweep(owner, at_distance(d - lag))
+
+        @pl.when(d < lag)
+        def _():
+            sweep(owner, None)
+
         out_copy(owner).start()
-        pltpu.make_async_copy(halves(owner, core), halves(owner, core), sk_recv.at[owner]).wait()
-        mate_copy(owner).start()
+        for extra in reversed(range(ahead)):
+            @pl.when((d * ahead - extra <= ahead * ahead) & (d * ahead - extra < n_t))
+            def _():
+                forward(d * ahead - extra)
+
+        @pl.when((d > ahead) & (d + ahead < n_t))
+        def _():
+            forward(d + ahead)
+
         return carry
 
     lax.fori_loop(1, n_t, visit, 0)
-    last = (t + 1) % n_t
-    pltpu.make_async_copy(halves(last, 1 - core), halves(last, 1 - core), mate_recv.at[last]).wait()
-
-    def finish(index, carry):
-        at = pl.ds(pl.multiple_of(index * chunk, chunk), chunk)
-        sketched_ref[at, :] += lax.dot_general(
-            kernel_all[last, at, :], columns[last], (((1,), (1,)), ((), ())), preferred_element_type=F32)
+
+    def finish(d, carry):
+        owner = at_distance(d)
+        complete(d)
+
+        def step(index, inner):
+            at = pl.ds(pl.multiple_of(index * chunk, chunk), chunk)
+            sketched_ref[at, :] += lax.dot_general(
+                kernel_all[owner, at, :], columns[owner], (((1,), (1,)), ((), ())), preferred_element_type=F32)
+            return inner
+
+        lax.fori_loop(0, rows // chunk, step, 0)
         return carry
 
-    lax.fori_loop(0, rows // chunk, finish, 0)
+    lax.fori_loop(n_t - lag, n_t, finish, 0)
     sketched = sketched_ref[...]
     grams[s] = jnp.dot(sketched.T, sketched, precision=HIGHEST, preferred_element_type=F32)
 
@@ -175,7 +208,7 @@
     trace = jnp.sum(jnp.where(eye, gram, 0.0))
     work[...] = gram + jnp.where(eye, SHIFT_SCALE * trace / rank, 0.0)
     inverse[...] = jnp.where(eye, 1.0, 0.0)
-    size = 16
+    size = 32
     local = lax.broadcasted_iota(jnp.int32, (size, rank), 0)
     for first in range(0, rank, size):
         panel = work[first:first + size, :]
@@ -184,7 +217,6 @@
         for i in range(size):
             pivot = jnp.broadcast_to(cols[i][i:i + 1, :], (size, rank))
             scale = lax.rsqrt(pivot)
-            scale = scale * (1.5 - 0.5 * pivot * scale * scale)
             factor = jnp.where(local > i, cols[i] * scale, 0.0)
             panel_row = panel[i:i + 1, :] * scale
             inv_row = inv_panel[i:i + 1, :] * scale

time: 60.1 us -> 52.9 us (0.88); the launches traced: 59.1 us -> 52.7 us
  Pallas kernels: 56.8 us -> 50.4 us
    pallas_call x1, Pallas kernels: 36.1 us -> 30.5 us  [body(): pl.pallas_call(functools.partial(sketch_kernel, n_t, n_s, cluster), out_s...]
    pallas_call x1, Pallas kernels: 8.14 us -> 7.25 us  [body(): pl.pallas_call(functools.partial(basis_kernel, total_rows), out_shape=(ja...]
where the time goes in v2:
time: 52.9 us; the launch traced here: 52.7 us
  Pallas kernels  50.4 us (95%)
  local copies, waits for them, and re-layouts  1.67 us (3%)
  between operations  0.65 us (1%)
    pallas_call x1, Pallas kernels, body(): pl.pallas_call(functools.partial(sketch_kernel, n_t, n_s, cluster), out_s...  30.5 us
    pallas_call x1, Pallas kernels, body(): pl.pallas_call(functools.partial(project_kernel, n_t, n_s, 1.0 / total_ro...  12.6 us
    pallas_call x1, Pallas kernels, body(): pl.pallas_call(functools.partial(basis_kernel, total_rows), out_shape=(ja...  7.25 us
    unnamed x1, local copies, waits for them, and re-layouts  1.67 us

profile of v2, /device:TPU:24, one launch (start us, length us, event | category | flops | bytes accessed | tf_op | source)
XLA Modules:
  0.0 52.7 jit_solution(4855976672030474426)
XLA Ops:
  0.6 30.5 %sketch.1 = (bf16[8,1024,512]{2,1,0:T(8,128)(2,1)}, f32[1024,128]{1,0:T(8,128)}, f32[128,128]{1,0:T(8,128)}) custom-call(f32[3,8,1024]{2,1,0:T(8,128)} %targets_ref.1, f32[3,512]{1,0:T(4,128)} %points_ref.1, f32[1,512]{1,0:T(1,128)} %bitcast.4, bf16[128,512]{1,0:T(8,128)(2,1)} %sketch_ref.1, s32[8,32]{1,0:T(8,128)} %mask_ref.1), custom_call_target="tpu_custom_call" | custom-call | tf_op jit(solution)/shard_map/sketch/pallas_call | solution.py:327
  31.2 7.2 %basis.1 = (bf16[1024,128]{1,0:T(8,128)(2,1)}, bf16[128,1024]{1,0:T(8,128)(2,1)}) custom-call(f32[128,128]{1,0:T(8,128)} %get-tuple-element.7.gram_ref, f32[1024,128]{1,0:T(8,128)} %get-tuple-element.8.sketched_ref), custom_call_target="tpu_custom_call" | custom-call | tf_op jit(solution)/shard_map/basis/pallas_call | solution.py:349
  38.4 12.6 %project.1 = bf16[128,1024]{1,0:T(8,128)(2,1)} custom-call(bf16[128,1024]{1,0:T(8,128)(2,1)} %get-tuple-element.10.flipped_ref, bf16[8,1024,512]{2,1,0:T(8,128)(2,1)} %get-tuple-element.11.kernel_in), custom_call_target="tpu_custom_call" | custom-call | tf_op jit(solution)/shard_map/project/pallas_call | solution.py:362
  51.0 1.7 %copy.8 = bf16[1,128,1024]{2,1,0:T(8,128)(2,1)} copy(bf16[1,128,1024]{2,1,0:T(8,128)(2,1)} %bitcast.3) | data formatting | bytes 524288

commit v3 on v2

--- a/solution.py
+++ b/solution.py
@@ -69,22 +69,33 @@
     for d in range(1, n_t):
         half_copy(d).start()
 
+    def parts(values):
+        first = values.astype(BF16).astype(F32)
+        second = (values - first).astype(BF16).astype(F32)
+        return first, second, values - first - second
+
     lanes = 128
-    stacked = jnp.concatenate(
-        [targets_ref[0, pl.ds(t, 1), :], targets_ref[1, pl.ds(t, 1), :], targets_ref[2, pl.ds(t, 1), :],
-         jnp.zeros((5, rows), F32)], axis=0)
+    tx = targets_ref[0, pl.ds(t, 1), :] - 0.5
+    ty = targets_ref[1, pl.ds(t, 1), :] - 0.5
+    tz = targets_ref[2, pl.ds(t, 1), :] - 0.5
+    t1, t2, t3 = parts(jnp.concatenate(
+        [tx, ty, tz, jnp.ones_like(tx), tx * tx + ty * ty + tz * tz, jnp.zeros((3, rows), F32)], axis=0))
+    stacked = jnp.concatenate([t1, t1, t2, t2, t1, t3, jnp.zeros((80, rows), F32)], axis=0)
     for first in range(0, rows, 128):
-        block = jnp.concatenate([stacked[:, first:first + 128], jnp.zeros((120, 128), F32)], axis=0).T
-        for axis in range(3):
-            target_cols[axis, first:first + 128, :] = jnp.broadcast_to(block[:, axis:axis + 1], (128, lanes))
+        target_cols[first:first + 128, :] = stacked[:, first:first + 128].T.astype(BF16)
     sketched_ref[...] = jnp.zeros_like(sketched_ref)
 
     chunk = rows
-    sub = 64
+    sub = 128
 
     def sweep(owner, previous):
-        sx, sy, sz = packed[owner, 0:1, :], packed[owner, 1:2, :], packed[owner, 2:3, :]
+        sx, sy, sz = packed[owner, 0:1, :] - 0.5, packed[owner, 1:2, :] - 0.5, packed[owner, 2:3, :] - 0.5
         charge = packed[owner, 3:4, :]
+        s1, s2, s3 = parts(jnp.concatenate(
+            [-2.0 * sx, -2.0 * sy, -2.0 * sz, sx * sx + sy * sy + sz * sz + SOFTENING,
+             jnp.ones_like(sx), jnp.zeros((3, width), F32)], axis=0))
+        features = jnp.concatenate(
+            [s1, s2, s1, s2, s3, s1, jnp.zeros((80, width), F32)], axis=0).astype(BF16)
         weights = []
         for piece in range(width // lanes):
             near = mask_ref[t, owner * (width // cluster) + piece * lanes // cluster]
@@ -94,14 +105,10 @@
             base = pl.multiple_of(index * chunk, chunk)
             for inner in range(chunk // sub):
                 at = pl.ds(base + inner * sub, sub)
-                tx, ty, tz = target_cols[0, at, :], target_cols[1, at, :], target_cols[2, at, :]
+                distance2 = jnp.dot(target_cols[at, :], features, preferred_element_type=F32)
                 for piece in range(width // lanes):
                     cut = slice(piece * lanes, (piece + 1) * lanes)
-                    dx = tx - sx[:, cut]
-                    dy = ty - sy[:, cut]
-                    dz = tz - sz[:, cut]
-                    distance2 = dx * dx + dy * dy + dz * dz + SOFTENING
-                    kernel_all[owner, at, cut] = (weights[piece] * lax.rsqrt(distance2)).astype(BF16)
+                    kernel_all[owner, at, cut] = (weights[piece] * lax.rsqrt(distance2[:, cut])).astype(BF16)
             if previous is not None:
                 at = pl.ds(base, chunk)
                 sketched_ref[at, :] += lax.dot_general(
@@ -337,7 +344,7 @@
             pltpu.VMEM((n_t, 4, width), F32),
             pltpu.VMEM((n_t, rank, width), BF16),
             pltpu.VMEM((n_t, rows, width), BF16),
-            pltpu.VMEM((3, rows, 128), F32),
+            pltpu.VMEM((rows, 128), BF16),
             pltpu.VMEM((n_s, rank, rank), F32),
             dma((n_t,)), dma((n_t,)), dma((n_t,)), dma((n_t,)), dma((n_t,)), dma((n_t,)),
             dma((n_s,)), dma((n_s,)), dma((n_t,)),

time: 52.9 us -> 51 us (0.964)
  Pallas kernels: 50.4 us -> 48.5 us
    pallas_call x1, Pallas kernels: 30.5 us -> 28.7 us  [body(): pl.pallas_call(functools.partial(sketch_kernel, n_t, n_s, cluster), out_s...]
where the time goes in v3:
time: 51 us; the launch traced here: 50.8 us
  Pallas kernels  48.5 us (95%)
  local copies, waits for them, and re-layouts  1.67 us (3%)
  between operations  0.65 us (1%)
    pallas_call x1, Pallas kernels, body(): pl.pallas_call(functools.partial(sketch_kernel, n_t, n_s, cluster), out_s...  28.7 us
    pallas_call x1, Pallas kernels, body(): pl.pallas_call(functools.partial(project_kernel, n_t, n_s, 1.0 / total_ro...  12.6 us
    pallas_call x1, Pallas kernels, body(): pl.pallas_call(functools.partial(basis_kernel, total_rows), out_shape=(ja...  7.24 us
    unnamed x1, local copies, waits for them, and re-layouts  1.67 us

profile of v3, /device:TPU:24, one launch (start us, length us, event | category | flops | bytes accessed | tf_op | source)
XLA Modules:
  0.0 50.8 jit_solution(12525508587879599474)
XLA Ops:
  0.6 28.7 %sketch.1 = (bf16[8,1024,512]{2,1,0:T(8,128)(2,1)}, f32[1024,128]{1,0:T(8,128)}, f32[128,128]{1,0:T(8,128)}) custom-call(f32[3,8,1024]{2,1,0:T(8,128)} %targets_ref.1, f32[3,512]{1,0:T(4,128)} %points_ref.1, f32[1,512]{1,0:T(1,128)} %bitcast.4, bf16[128,512]{1,0:T(8,128)(2,1)} %sketch_ref.1, s32[8,32]{1,0:T(8,128)} %mask_ref.1), custom_call_target="tpu_custom_call" | custom-call | tf_op jit(solution)/shard_map/sketch/pallas_call | solution.py:334
  29.3 7.2 %basis.1 = (bf16[1024,128]{1,0:T(8,128)(2,1)}, bf16[128,1024]{1,0:T(8,128)(2,1)}) custom-call(f32[128,128]{1,0:T(8,128)} %get-tuple-element.7.gram_ref, f32[1024,128]{1,0:T(8,128)} %get-tuple-element.8.sketched_ref), custom_call_target="tpu_custom_call" | custom-call | tf_op jit(solution)/shard_map/basis/pallas_call | solution.py:356
  36.5 12.6 %project.1 = bf16[128,1024]{1,0:T(8,128)(2,1)} custom-call(bf16[128,1024]{1,0:T(8,128)(2,1)} %get-tuple-element.10.flipped_ref, bf16[8,1024,512]{2,1,0:T(8,128)(2,1)} %get-tuple-element.11.kernel_in), custom_call_target="tpu_custom_call" | custom-call | tf_op jit(solution)/shard_map/project/pallas_call | solution.py:369
  49.1 1.7 %copy.8 = bf16[1,128,1024]{2,1,0:T(8,128)(2,1)} copy(bf16[1,128,1024]{2,1,0:T(8,128)(2,1)} %bitcast.3) | data formatting | bytes 524288
